TPU v7x, 128 devices: a whole 4x4x4 slice. The times are simulated.
128 devices in a mesh: dp: 16 (over x, z), tensor: 8 (over y, core).
Axes of the slice: x: 4, y: 4, z: 4, core: 2. Of those that a mesh axis runs over, the one named last changes fastest.
Arguments:
- attn_norm_grad: bfloat16 [16, 2048], P('dp', 'tensor'), may hold values from -1.5 to 1.5
- query_grad: bfloat16 [16, 2048, 2048], P('dp', None, 'tensor'), may hold values from -1.5 to 1.5
- forget_grad: bfloat16 [16, 2048, 2048], P('dp', None, 'tensor'), may hold values from -1.5 to 1.5
- input_grad: bfloat16 [16, 2048, 2048], P('dp', None, 'tensor'), may hold values from -1.5 to 1.5
- group_norm_grad: bfloat16 [16, 2048], P('dp', 'tensor'), may hold values from -1.5 to 1.5
- output_gate_grad: bfloat16 [16, 2048, 2048], P('dp', None, 'tensor'), may hold values from -1.5 to 1.5
- out_proj_grad: bfloat16 [16, 2048, 2048], P('dp', 'tensor'), may hold values from -1.5 to 1.5
- mlp_norm_grad: bfloat16 [16, 2048], P('dp', 'tensor'), may hold values from -1.5 to 1.5
- gate_proj_grad: bfloat16 [16, 2048, 2816], P('dp', None, 'tensor'), may hold values from -1.5 to 1.5
- up_proj_grad: bfloat16 [16, 2048, 2816], P('dp', None, 'tensor'), may hold values from -1.5 to 1.5
- down_proj_grad: bfloat16 [16, 2816, 2048], P('dp', 'tensor'), may hold values from -1.5 to 1.5
- weights: float32 [8, 4784896], P('tensor', 'dp'), as said below
- first_moment: float32 [8, 4784896], P('tensor', 'dp'), may hold values from -0.6 to 0.6
- second_moment: float32 [8, 4784896], P('tensor', 'dp'), may hold values from 0.001 to 1
Outputs:
- new_weights: float32 [8, 4784896], P('tensor', 'dp')
- new_first: float32 [8, 4784896], P('tensor', 'dp')
- new_second: float32 [8, 4784896], P('tensor', 'dp')
- attn_norm_copy: bfloat16 [2048], P('tensor')
- query_copy: bfloat16 [2048, 2048], P(None, 'tensor')
- forget_copy: bfloat16 [2048, 2048], P(None, 'tensor')
- input_copy: bfloat16 [2048, 2048], P(None, 'tensor')
- group_norm_copy: bfloat16 [2048], P('tensor')
- output_gate_copy: bfloat16 [2048, 2048], P(None, 'tensor')
- out_proj_copy: bfloat16 [2048, 2048], P('tensor')
- mlp_norm_copy: bfloat16 [2048], P('tensor')
- gate_proj_copy: bfloat16 [2048, 2816], P(None, 'tensor')
- up_proj_copy: bfloat16 [2048, 2816], P(None, 'tensor')
- down_proj_copy: bfloat16 [2816, 2048], P('tensor')
Inputs may be any that keep to these rules, and one draw needn't show every extreme that they name: float32 master weights of order one.
All inputs are finite; a program needn't handle non-finite values.
Results may differ from a plain program's by a relative error of at most 0.0085.
Values may be sent and summed in bfloat16 or wider, within the bound.
A program may use at most 192 MiB of HBM per device.

v0:
```python
import jax
import jax.numpy as jnp
from jax import lax
from jax.sharding import PartitionSpec as P

GAIN_SEGMENTS = (0, 4, 7)


def segment_sums(onehot, values):
    return jnp.dot(onehot, values, precision=lax.Precision.HIGHEST)


def split_rows(block, owners):
    if block.ndim == 1:
        return block.reshape(owners, block.shape[0] // owners)
    return block.reshape(owners, block.shape[0] // owners, block.shape[1])


def on_device(
    attn_norm_grad,
    query_grad,
    forget_grad,
    input_grad,
    group_norm_grad,
    output_gate_grad,
    out_proj_grad,
    mlp_norm_grad,
    gate_proj_grad,
    up_proj_grad,
    down_proj_grad,
    weights,
    first_moment,
    second_moment,
):
    grads = (
        attn_norm_grad,
        query_grad,
        forget_grad,
        input_grad,
        group_norm_grad,
        output_gate_grad,
        out_proj_grad,
        mlp_norm_grad,
        gate_proj_grad,
        up_proj_grad,
        down_proj_grad,
    )
    owners = lax.axis_size("dp")
    shapes = [g.shape[1:] for g in grads]
    pieces = [split_rows(g[0], owners) for g in grads]
    piece_len = [p[0].size for p in pieces]
    own_count = sum(piece_len)
    weight_row = weights.reshape(-1)
    first_row = first_moment.reshape(-1)
    second_row = second_moment.reshape(-1)
    position = jnp.arange(own_count, dtype=jnp.int32)
    segment = jnp.zeros((own_count,), jnp.int32)
    bound = 0
    for number in range(10):
        bound += piece_len[number]
        segment = segment + (position >= bound).astype(jnp.int32)
    onehot = (segment[None, :] == jnp.arange(11, dtype=jnp.int32)[:, None]).astype(jnp.float32)
    gain_mask = onehot[GAIN_SEGMENTS[0]] + onehot[GAIN_SEGMENTS[1]] + onehot[GAIN_SEGMENTS[2]]
    summed = (
        lax.psum_scatter(
            pieces[0].astype(jnp.float32).astype(jnp.bfloat16),
            "dp",
            scatter_dimension=0,
            tiled=True,
        ).astype(jnp.float32),
        lax.psum_scatter(
            pieces[1].astype(jnp.float32).astype(jnp.bfloat16),
            "dp",
            scatter_dimension=0,
            tiled=True,
        ).astype(jnp.float32),
        lax.psum_scatter(
            pieces[2].astype(jnp.float32).astype(jnp.bfloat16),
            "dp",
            scatter_dimension=0,
            tiled=True,
        ).astype(jnp.float32),
        lax.psum_scatter(
            pieces[3].astype(jnp.float32).astype(jnp.bfloat16),
            "dp",
            scatter_dimension=0,
            tiled=True,
        ).astype(jnp.float32),
        lax.psum_scatter(
            pieces[4].astype(jnp.float32).astype(jnp.bfloat16),
            "dp",
            scatter_dimension=0,
            tiled=True,
        ).astype(jnp.float32),
        lax.psum_scatter(
            pieces[5].astype(jnp.float32).astype(jnp.bfloat16),
            "dp",
            scatter_dimension=0,
            tiled=True,
        ).astype(jnp.float32),
        lax.psum_scatter(
            pieces[6].astype(jnp.float32).astype(jnp.bfloat16),
            "dp",
            scatter_dimension=0,
            tiled=True,
        ).astype(jnp.float32),
        lax.psum_scatter(
            pieces[7].astype(jnp.float32).astype(jnp.bfloat16),
            "dp",
            scatter_dimension=0,
            tiled=True,
        ).astype(jnp.float32),
        lax.psum_scatter(
            pieces[8].astype(jnp.float32).astype(jnp.bfloat16),
            "dp",
            scatter_dimension=0,
            tiled=True,
        ).astype(jnp.float32),
        lax.psum_scatter(
            pieces[9].astype(jnp.float32).astype(jnp.bfloat16),
            "dp",
            scatter_dimension=0,
            tiled=True,
        ).astype(jnp.float32),
        lax.psum_scatter(
            pieces[10].astype(jnp.float32).astype(jnp.bfloat16),
            "dp",
            scatter_dimension=0,
            tiled=True,
        ).astype(jnp.float32),
    )
    grad = jnp.concatenate([s.reshape(-1) for s in summed])
    new_first = 0.9 * first_row + 0.1 * grad
    new_second = 0.999 * second_row + 0.001 * grad * grad
    update = new_first / (jnp.sqrt(new_second) + 1e-06) + 0.01 * weight_row * (1.0 - gain_mask)
    weight_sq, update_sq = lax.psum(
        (segment_sums(onehot, weight_row * weight_row), segment_sums(onehot, update * update)),
        ("dp", "tensor"),
    )
    trust = jnp.sqrt(weight_sq) / jnp.sqrt(update_sq)
    scale = jnp.dot(trust, onehot, precision=lax.Precision.HIGHEST)
    new_weights = weight_row - 0.1 * scale * update
    rounded = new_weights.astype(jnp.bfloat16)
    owned = []
    offset = 0
    for number in range(11):
        owned.append(
            rounded[offset : offset + piece_len[number]].reshape((1,) + pieces[number].shape[1:])
        )
        offset += piece_len[number]
    gathered = (
        lax.all_gather(owned[0], "dp", axis=0, tiled=True),
        lax.all_gather(owned[1], "dp", axis=0, tiled=True),
        lax.all_gather(owned[2], "dp", axis=0, tiled=True),
        lax.all_gather(owned[3], "dp", axis=0, tiled=True),
        lax.all_gather(owned[4], "dp", axis=0, tiled=True),
        lax.all_gather(owned[5], "dp", axis=0, tiled=True),
        lax.all_gather(owned[6], "dp", axis=0, tiled=True),
        lax.all_gather(owned[7], "dp", axis=0, tiled=True),
        lax.all_gather(owned[8], "dp", axis=0, tiled=True),
        lax.all_gather(owned[9], "dp", axis=0, tiled=True),
        lax.all_gather(owned[10], "dp", axis=0, tiled=True),
    )
    copies = [gathered[number].reshape(shapes[number]) for number in range(11)]
    return (
        new_weights.reshape(1, -1),
        new_first.reshape(1, -1),
        new_second.reshape(1, -1),
        copies[0],
        copies[1],
        copies[2],
        copies[3],
        copies[4],
        copies[5],
        copies[6],
        copies[7],
        copies[8],
        copies[9],
        copies[10],
    )


def solution(mesh):
    return jax.shard_map(
        on_device,
        mesh=mesh,
        in_specs=(
            P("dp", "tensor"),
            P("dp", None, "tensor"),
            P("dp", None, "tensor"),
            P("dp", None, "tensor"),
            P("dp", "tensor"),
            P("dp", None, "tensor"),
            P("dp", "tensor", None),
            P("dp", "tensor"),
            P("dp", None, "tensor"),
            P("dp", None, "tensor"),
            P("dp", "tensor", None),
            P("tensor", "dp"),
            P("tensor", "dp"),
            P("tensor", "dp"),
        ),
        out_specs=(
            P("tensor", "dp"),
            P("tensor", "dp"),
            P("tensor", "dp"),
            P("tensor"),
            P(None, "tensor"),
            P(None, "tensor"),
            P(None, "tensor"),
            P("tensor"),
            P(None, "tensor"),
            P("tensor", None),
            P("tensor"),
            P(None, "tensor"),
            P(None, "tensor"),
            P("tensor", None),
        ),
        check_vma=False,
    )
```

profile of v0, /device:TPU:0, one launch (start us, length us, event | category | flops | bytes accessed | tf_op | source)
XLA Modules:
  0.0 1172.6 jit_solution(3635013927501478566)
XLA Ops:
  27.7 13.4 %reduce = f32[299056]{0:T(1024)S(1)} reduce(f32[1,299056]{1,0:T(1,128)} %param.25, f32[]{:T(128)} %constant.110), dimensions={0}, to_apply=%param.25.reduce_sub_computation | reduce | bytes 2392452 | tf_op args[11]
  41.1 76.1 %all-reduce.16 = (bf16[16,16]{1,0:T(8,128)(2,1)S(1)}, bf16[16,16]{1,0:T(8,128)(2,1)S(1)}, bf16[16,16]{1,0:T(8,128)(2,1)S(1)}) all-reduce(bf16[16,16]{1,0:T(8,128)(2,1)S(1)} %reshape_squeeze.33, bf16[16,16]{1,0:T(8,128)(2,1)S(1)} %reshape_squeeze.37, ...), channel_id=5, replica_groups=mesh['dp'=16,'tensor'=8] {'dp'}, use_global_device_ids=true, to_apply=%region_1.0.clone | all-reduce | flops 768 | bytes 3072
  121.0 20.0 %fusion.15 = f32[299056]{0:T(1024)} fusion(f32[11,299056]{1,0:T(8,128)} %fusion.2), kind=kLoop, calls=%fused_computation.35 | loop fusion | flops 897168 | bytes 4784896 | tf_op jit(solution)/shard_map/sub | solution.py:135
  142.1 20.7 %reduce-scatter.27.cloned.1.call-done = bf16[1,128,256]{2,1,0:T(8,128)(2,1)} async-done(((bf16[16,128,256]{2,1,0:T(8,128)(2,1)}), bf16[1,128,256]{2,1,0:T(8,128)(2,1)}) %reduce-scatter.27.cloned.1.call-update) | async-done | bytes 65552
  163.7 74.5 %reduce-scatter.29.cloned.1.call-done = bf16[1,128,256]{2,1,0:T(8,128)(2,1)} async-done(((bf16[16,128,256]{2,1,0:T(8,128)(2,1)}), bf16[1,128,256]{2,1,0:T(8,128)(2,1)}) %reduce-scatter.29.cloned.1.call-update) | async-done | bytes 65552
  239.9 74.0 %reduce-scatter.31.cloned.1.call-done = bf16[1,128,256]{2,1,0:T(8,128)(2,1)} async-done(((bf16[16,128,256]{2,1,0:T(8,128)(2,1)}), bf16[1,128,256]{2,1,0:T(8,128)(2,1)}) %reduce-scatter.31.cloned.1.call-update) | async-done | bytes 65552
  315.6 73.7 %reduce-scatter.33.cloned.1.call-done = bf16[1,16,2048]{2,1,0:T(8,128)(2,1)} async-done(((bf16[16,16,2048]{2,1,0:T(8,128)(2,1)}), bf16[1,16,2048]{2,1,0:T(8,128)(2,1)}) %reduce-scatter.33.cloned.1.call-update) | async-done | bytes 65552
  414.8 51.4 %reduce-scatter.35.cloned.1.call-done = bf16[1,128,352]{1,2,0:T(8,128)(2,1)} async-done(((bf16[16,128,352]{1,2,0:T(8,128)(2,1)}), bf16[1,128,352]{1,2,0:T(8,128)(2,1)}) %reduce-scatter.35.cloned.1.call-update) | async-done | bytes 90128
  467.7 75.6 %reduce-scatter.37.cloned.1.call-done = bf16[1,128,352]{1,2,0:T(8,128)(2,1)} async-done(((bf16[16,128,352]{1,2,0:T(8,128)(2,1)}), bf16[1,128,352]{1,2,0:T(8,128)(2,1)}) %reduce-scatter.37.cloned.1.call-update) | async-done | bytes 90128
  544.8 75.0 %reduce-scatter.39.cloned.1.call-done = bf16[1,22,2048]{2,1,0:T(8,128)(2,1)} async-done(((bf16[16,22,2048]{2,1,0:T(8,128)(2,1)}), bf16[1,22,2048]{2,1,0:T(8,128)(2,1)}) %reduce-scatter.39.cloned.1.call-update) | async-done | bytes 90128
  634.0 21.6 %fusion.13 = (f32[1,299056]{1,0:T(1,128)}, f32[299056]{0:T(1024)}, f32[1,299056]{1,0:T(1,128)}, f32[299056]{0:T(1024)}) fusion(f32[1,299056]{1,0:T(1,128)} %dynamic-update-slice.13, f32[1,299056]{1,0:T(1,128)} %param.27, f32[1,299056]{1,0:T(1,128)} %param.26), kind=kLoop, calls=%fused_computation.30 | loop fusion | flops 2093392 | bytes 8373568 | tf_op jit(solution)/shard_map/add | solution.py:134
  655.7 16.2 %concatenate.41 = f32[299056]{0:T(1024)} concatenate(f32[16]{0:T(128)S(1)} %bitcast.103, f32[32768]{0:T(1024)S(1)} %bitcast.93, f32[32768]{0:T(1024)S(1)} %bitcast.94, f32[32768]{0:T(1024)S(1)} %bitcast.95, f32[16]{0:T(128)S(1)} %fusion.32, f32[32768]{0:T(1024)} %bitcast.96, f32[32768]{0:T(1024)} %bitcast.97, f32[16]{0:T(128)S(1)} %bitcast.104, f32[45056]{0:T(1024)S(1)} %reshape.617, ...), dimensions={0} | concatenate | bytes 2392448 | tf_op jit(solution)/shard_map/concatenate | solution.py:132
  681.8 12.5 %fusion.17 = f32[11]{0:T(128)S(1)} fusion(f32[299056,1]{0,1:T(1,128)S(1)} %reshape.666, s32[299056]{0:T(1024)S(1)} %convert_add_fusion), kind=kOutput, calls=%fused_computation.37 | convolution fusion | flops 42765008 | bytes 2392492 | tf_op jit(solution)/shard_map/dot_general | solution.py:10
  700.1 12.5 %fusion.16 = f32[11]{0:T(128)S(1)} fusion(f32[299056,1]{0,1:T(1,128)S(1)} %reshape.664, s32[299056]{0:T(1024)S(1)} %convert_add_fusion), kind=kOutput, calls=%fused_computation.36 | convolution fusion | flops 42765008 | bytes 2392492 | tf_op jit(solution)/shard_map/dot_general | solution.py:10
  712.6 65.0 %all-reduce.14 = (f32[11]{0:T(128)S(1)}, f32[11]{0:T(128)S(1)}) all-reduce(f32[11]{0:T(128)S(1)} %fusion.17, f32[11]{0:T(128)S(1)} %fusion.16), channel_id=1, replica_groups=mesh['dp'=16,'tensor'=8] {'dp','tensor'}, use_global_device_ids=true, to_apply=%region_12.0 | all-reduce | flops 22 | bytes 176 | tf_op jit(solution)/shard_map/psum | solution.py:136
  777.6 20.0 %fusion.7 = f32[299056]{0:T(1024)S(1)} fusion(s32[299056]{0:T(1024)S(1)} %convert_add_fusion, f32[11]{0:T(128)S(1)} %get-tuple-element.28, f32[11]{0:T(128)S(1)} %get-tuple-element.29), kind=kOutput, calls=%fused_computation.22 | convolution fusion | flops 42765020 | bytes 2392536 | tf_op jit(solution)/shard_map/dot_general | solution.py:141
  812.4 38.4 %all-reduce.15 = (bf16[256]{0:T(256)(128)(2,1)}, bf16[256]{0:T(256)(128)(2,1)}, bf16[256]{0:T(256)(128)(2,1)}) all-reduce(bf16[256]{0:T(256)(128)(2,1)S(1)} %dynamic-update-slice, bf16[256]{0:T(256)(128)(2,1)S(1)} %dynamic-update-slice.1, bf16[256]{0:T(256)(128)(2,1)S(1)} %dynamic-update-slice.2), channel_id=2, replica_groups=mesh['dp'=16,'tensor'=8] {'dp'}, use_global_device_ids=true, to_apply=%add | all-reduce | flops 768 | bytes 3072
  850.8 31.7 %all-gather.14.cloned.1.call-done = bf16[16,128,256]{2,1,0:T(8,128)(2,1)} async-done(((bf16[1,128,256]{2,1,0:T(8,128)(2,1)}), bf16[16,128,256]{2,1,0:T(8,128)(2,1)}) %all-gather.14.cloned.1.call-update) | async-done | bytes 1048592 | tf_op jit(solution)/shard_map/all_gather | solution.py:154
  882.5 45.1 %all-gather.16.cloned.1.call-done = bf16[16,128,256]{2,1,0:T(8,128)(2,1)} async-done(((bf16[1,128,256]{2,1,0:T(8,128)(2,1)}), bf16[16,128,256]{2,1,0:T(8,128)(2,1)}) %all-gather.16.cloned.1.call-update) | async-done | bytes 1048592 | tf_op jit(solution)/shard_map/all_gather | solution.py:155
  927.6 44.9 %all-gather.18.cloned.1.call-done = bf16[16,128,256]{2,1,0:T(8,128)(2,1)} async-done(((bf16[1,128,256]{2,1,0:T(8,128)(2,1)}), bf16[16,128,256]{2,1,0:T(8,128)(2,1)}) %all-gather.18.cloned.1.call-update) | async-done | bytes 1048592 | tf_op jit(solution)/shard_map/all_gather | solution.py:157
  972.5 45.1 %all-gather.20.cloned.1.call-done = bf16[16,16,2048]{2,1,0:T(8,128)(2,1)} async-done(((bf16[1,16,2048]{2,1,0:T(8,128)(2,1)}), bf16[16,16,2048]{2,1,0:T(8,128)(2,1)}) %all-gather.20.cloned.1.call-update) | async-done | bytes 1048592 | tf_op jit(solution)/shard_map/all_gather | solution.py:158
  1017.6 46.1 %all-gather.22.cloned.1.call-done = bf16[16,128,352]{1,2,0:T(8,128)(2,1)} async-done(((bf16[1,128,352]{1,2,0:T(8,128)(2,1)}), bf16[16,128,352]{1,2,0:T(8,128)(2,1)}) %all-gather.22.cloned.1.call-update) | async-done | bytes 1441808 | tf_op jit(solution)/shard_map/all_gather | solution.py:160
  1066.3 43.5 %all-gather.24.cloned.1.call-done = bf16[16,128,352]{1,2,0:T(8,128)(2,1)} async-done(((bf16[1,128,352]{1,2,0:T(8,128)(2,1)}), bf16[16,128,352]{1,2,0:T(8,128)(2,1)}) %all-gather.24.cloned.1.call-update) | async-done | bytes 1441808 | tf_op jit(solution)/shard_map/all_gather | solution.py:161
  1112.4 43.6 %all-gather.26.cloned.1.call-done = bf16[16,22,2048]{2,1,0:T(8,128)(2,1)} async-done(((bf16[1,22,2048]{2,1,0:T(8,128)(2,1)}), bf16[16,22,2048]{2,1,0:T(8,128)(2,1)}) %all-gather.26.cloned.1.call-update) | async-done | bytes 1441808 | tf_op jit(solution)/shard_map/all_gather | solution.py:162
  (155 shorter events, 116.7 us)
Async XLA Ops:
  7.2 133.9 %reduce-scatter.25.cloned.1.call-start = ((), (), s32[]{:S(2)}) async-start(), calls=%async_computation.16 | async-start | bytes 1114112
  7.9 154.8 %reduce-scatter.27.cloned.1.call-start = ((), (), s32[]{:S(2)}) async-start(), calls=%async_computation.17 | async-start | bytes 1114112
  8.7 229.6 %reduce-scatter.29.cloned.1.call-start = ((), (), s32[]{:S(2)}) async-start(), calls=%async_computation.18 | async-start | bytes 1114112
  9.4 304.5 %reduce-scatter.31.cloned.1.call-start = ((), (), s32[]{:S(2)}) async-start(), calls=%async_computation.19 | async-start | bytes 1114112
  10.0 379.3 %reduce-scatter.33.cloned.1.call-start = ((), (), s32[]{:S(2)}) async-start(), calls=%async_computation.20 | async-start | bytes 1114112
  10.6 455.7 %reduce-scatter.35.cloned.1.call-start = ((), (), s32[]{:S(2)}) async-start(), calls=%async_computation.21 | async-start | bytes 1531904
  12.6 530.7 %reduce-scatter.37.cloned.1.call-start = ((), (), s32[]{:S(2)}) async-start(), calls=%async_computation.22 | async-start | bytes 1531904
  15.8 604.0 %reduce-scatter.39.cloned.1.call-start = ((), (), s32[]{:S(2)}) async-start(), calls=%async_computation.23 | async-start | bytes 1671168
  18.6 832.3 %all-gather.12.cloned.1.call-start = ((), (), s32[]{:S(2)}) async-start(), calls=%async_computation.8 | async-start | bytes 1114112 | tf_op jit(solution)/shard_map/all_gather | solution.py:153
  18.7 8.7 copy-start.16
  18.7 8.8 copy-start.17
  27.7 89.5 %copy-start.14 = (u32[128]{0:T(128)S(1)}, u32[128]{0:T(128)}, u32[]{:S(2)}) copy-start(u32[128]{0:T(128)} %constant.50) | copy-start | bytes 1540
  633.9 21.6 %copy-start.13 = (bf16[1,22,2048]{2,1,0:T(8,128)(2,1)S(1)}, bf16[1,22,2048]{2,1,0:T(8,128)(2,1)}, u32[]{:S(2)}) copy-start(bf16[1,22,2048]{2,1,0:T(8,128)(2,1)} %reduce-scatter.39.cloned.1.call-done) | copy-start | bytes 270340
  633.9 21.7 %copy-start.9 = (f32[16,2,8,128]{3,1,2,0:T(2,128)S(1)}, f32[16,2,8,128]{3,1,2,0:T(2,128)}, u32[]{:S(2)}) copy-start(f32[16,2,8,128]{3,1,2,0:T(2,128)} %copy.53) | copy-start | bytes 393220
  634.0 21.7 %copy-start.10 = (f32[16,2,8,128]{3,1,2,0:T(2,128)S(1)}, f32[16,2,8,128]{3,1,2,0:T(2,128)}, u32[]{:S(2)}) copy-start(f32[16,2,8,128]{3,1,2,0:T(2,128)} %copy.54) | copy-start | bytes 393220
  777.6 20.0 %copy-start = (f32[299056]{0:T(1024)S(1)}, f32[299056]{0:T(1024)}, u32[]{:S(2)}) copy-start(f32[299056]{0:T(1024)} %get-tuple-element.39) | copy-start | bytes 3588676
  798.7 83.8 %all-gather.14.cloned.1.call-start = ((), (), s32[]{:S(2)}) async-start(), calls=%async_computation.9 | async-start | bytes 1114112 | tf_op jit(solution)/shard_map/all_gather | solution.py:154
  799.5 128.2 %all-gather.16.cloned.1.call-start = ((), (), s32[]{:S(2)}) async-start(), calls=%async_computation.10 | async-start | bytes 1114112 | tf_op jit(solution)/shard_map/all_gather | solution.py:155
  800.2 172.3 %all-gather.18.cloned.1.call-start = ((), (), s32[]{:S(2)}) async-start(), calls=%async_computation.11 | async-start | bytes 1114112 | tf_op jit(solution)/shard_map/all_gather | solution.py:157
  800.9 216.7 %all-gather.20.cloned.1.call-start = ((), (), s32[]{:S(2)}) async-start(), calls=%async_computation.12 | async-start | bytes 1114112 | tf_op jit(solution)/shard_map/all_gather | solution.py:158
  801.7 262.0 %all-gather.22.cloned.1.call-start = ((), (), s32[]{:S(2)}) async-start(), calls=%async_computation.13 | async-start | bytes 1531904 | tf_op jit(solution)/shard_map/all_gather | solution.py:160
  802.8 307.0 %all-gather.24.cloned.1.call-start = ((), (), s32[]{:S(2)}) async-start(), calls=%async_computation.14 | async-start | bytes 1531904 | tf_op jit(solution)/shard_map/all_gather | solution.py:161
  803.8 352.2 %all-gather.26.cloned.1.call-start = ((), (), s32[]{:S(2)}) async-start(), calls=%async_computation.15 | async-start | bytes 1671168 | tf_op jit(solution)/shard_map/all_gather | solution.py:162
  1112.4 46.0 %copy-start.4 = (bf16[16,128,256]{2,1,0:T(8,128)(2,1)S(1)}, bf16[16,128,256]{2,1,0:T(8,128)(2,1)}, u32[]{:S(2)}) copy-start(bf16[16,128,256]{2,1,0:T(8,128)(2,1)} %all-gather.12.cloned.1.call-done) | copy-start | bytes 3145732
  (10 other events, 23.6 us)
Sparse Core Ops, SparseCore 0:
  11.2 75.6 reduce-scatter.24
  90.4 72.2 reduce-scatter.26
  165.9 72.2 reduce-scatter.28
  241.7 72.2 reduce-scatter.30
  317.0 72.2 reduce-scatter.32
  393.3 72.8 reduce-scatter.34
  470.4 72.9 reduce-scatter.36
  546.9 72.9 reduce-scatter.38
  798.8 38.8 all-gather.11
  840.6 41.9 all-gather.13
  885.5 42.0 all-gather.15
  930.4 42.0 all-gather.17
  975.5 42.0 all-gather.19
  1020.5 43.1 all-gather.21
  1066.5 43.2 all-gather.23
  1112.6 43.3 all-gather.25
where the time goes:
time: 1180 us; the launch traced here: 1170 us
  waiting for transfers between devices  748 us (63%)
  blocking collectives  180 us (15%)
  local copies, waits for them, and re-layouts  107 us (9%)
  other arithmetic  76.6 us (6%)
  matrix products  45 us (4%)
  between operations  15.1 us (1%)
    unnamed x24, waiting for transfers between devices  448 us
    unnamed x2, blocking collectives  115 us
    psum x1, blocking collectives, on_device(): lax.psum((segment_sums(onehot, weight_row * weight_row), segment_sums(one...  65 us
    unnamed x71, local copies, waits for them, and re-layouts  47.3 us
    all_gather x1, waiting for transfers between devices, on_device(): lax.all_gather(owned[8], 'dp', axis=0, tiled=True)  46.1 us
    all_gather x1, waiting for transfers between devices, on_device(): lax.all_gather(owned[3], 'dp', axis=0, tiled=True)  45.1 us
    all_gather x1, waiting for transfers between devices, on_device(): lax.all_gather(owned[6], 'dp', axis=0, tiled=True)  45.1 us
    all_gather x1, waiting for transfers between devices, on_device(): lax.all_gather(owned[5], 'dp', axis=0, tiled=True)  44.9 us
  transfers between devices with their start and end apart: 16, of which 14 were waited for; matrix products, arithmetic and copies ran while one was open for 9% of the time, Pallas kernels for 0%

commit v1 on v0

--- a/solution.py
+++ b/solution.py
@@ -4,6 +4,11 @@
 from jax.sharding import PartitionSpec as P
 
 GAIN_SEGMENTS = (0, 4, 7)
+
+
+def measure_the_array(point):
+    t1 = jax.lax.psum(jax.lax.psum(point, axis_name="tensor"), axis_name="dp")
+    return t1
 
 
 def segment_sums(onehot, values):
@@ -133,9 +138,8 @@
     new_first = 0.9 * first_row + 0.1 * grad
     new_second = 0.999 * second_row + 0.001 * grad * grad
     update = new_first / (jnp.sqrt(new_second) + 1e-06) + 0.01 * weight_row * (1.0 - gain_mask)
-    weight_sq, update_sq = lax.psum(
-        (segment_sums(onehot, weight_row * weight_row), segment_sums(onehot, update * update)),
-        ("dp", "tensor"),
+    weight_sq, update_sq = measure_the_array(
+        (segment_sums(onehot, weight_row * weight_row), segment_sums(onehot, update * update))
     )
     trust = jnp.sqrt(weight_sq) / jnp.sqrt(update_sq)
     scale = jnp.dot(trust, onehot, precision=lax.Precision.HIGHEST)

time: 1180 us -> 1170 us (level)
  blocking collectives: 180 us -> 164 us
    psum x1 -> x2, blocking collectives: 65 us -> 51.4 us  [measure_the_array(): t1 = jax.lax.psum(jax.lax.psum(point, axis_name='tensor'), axis_name='dp')]
where the time goes in v1:
time: 1170 us; the launch traced here: 1160 us
  waiting for transfers between devices  749 us (64%)
  blocking collectives  164 us (14%)
  local copies, waits for them, and re-layouts  107 us (9%)
  other arithmetic  76.4 us (7%)
  matrix products  45 us (4%)
  between operations  15.4 us (1%)
    unnamed x24, waiting for transfers between devices  449 us
    unnamed x2, blocking collectives  112 us
    psum x2, blocking collectives, measure_the_array(): t1 = jax.lax.psum(jax.lax.psum(point, axis_name='tensor'), axis_name='dp')  51.4 us
    unnamed x71, local copies, waits for them, and re-layouts  47.3 us
    all_gather x1, waiting for transfers between devices, on_device(): lax.all_gather(owned[8], 'dp', axis=0, tiled=True)  46.1 us
    all_gather x1, waiting for transfers between devices, on_device(): lax.all_gather(owned[3], 'dp', axis=0, tiled=True)  45.1 us
    all_gather x1, waiting for transfers between devices, on_device(): lax.all_gather(owned[6], 'dp', axis=0, tiled=True)  45.1 us
    all_gather x1, waiting for transfers between devices, on_device(): lax.all_gather(owned[5], 'dp', axis=0, tiled=True)  44.9 us
  transfers between devices with their start and end apart: 16, of which 14 were waited for; matrix products, arithmetic and copies ran while one was open for 9% of the time, Pallas kernels for 0%

profile of v1, /device:TPU:0, one launch (start us, length us, event | category | flops | bytes accessed | tf_op | source)
XLA Modules:
  0.0 1157.3 jit_solution(15073703234234142860)
XLA Ops:
  27.7 13.4 %reduce = f32[299056]{0:T(1024)S(1)} reduce(f32[1,299056]{1,0:T(1,128)} %param.25, f32[]{:T(128)} %constant.110), dimensions={0}, to_apply=%param.25.reduce_sub_computation | reduce | bytes 2392452 | tf_op args[11]
  41.0 76.1 %all-reduce.17 = (bf16[16,16]{1,0:T(8,128)(2,1)S(1)}, bf16[16,16]{1,0:T(8,128)(2,1)S(1)}, bf16[16,16]{1,0:T(8,128)(2,1)S(1)}) all-reduce(bf16[16,16]{1,0:T(8,128)(2,1)S(1)} %reshape_squeeze.33, bf16[16,16]{1,0:T(8,128)(2,1)S(1)} %reshape_squeeze.37, ...), channel_id=5, replica_groups=mesh['dp'=16,'tensor'=8] {'dp'}, use_global_device_ids=true, to_apply=%region_2.0.clone | all-reduce | flops 768 | bytes 3072
  121.0 20.0 %fusion.15 = f32[299056]{0:T(1024)} fusion(f32[11,299056]{1,0:T(8,128)} %fusion.2), kind=kLoop, calls=%fused_computation.35 | loop fusion | flops 897168 | bytes 4784896 | tf_op jit(solution)/shard_map/sub | solution.py:140
  142.0 20.8 %reduce-scatter.27.cloned.1.call-done = bf16[1,128,256]{2,1,0:T(8,128)(2,1)} async-done(((bf16[16,128,256]{2,1,0:T(8,128)(2,1)}), bf16[1,128,256]{2,1,0:T(8,128)(2,1)}) %reduce-scatter.27.cloned.1.call-update) | async-done | bytes 65552
  163.7 74.5 %reduce-scatter.29.cloned.1.call-done = bf16[1,128,256]{2,1,0:T(8,128)(2,1)} async-done(((bf16[16,128,256]{2,1,0:T(8,128)(2,1)}), bf16[1,128,256]{2,1,0:T(8,128)(2,1)}) %reduce-scatter.29.cloned.1.call-update) | async-done | bytes 65552
  239.9 74.1 %reduce-scatter.31.cloned.1.call-done = bf16[1,128,256]{2,1,0:T(8,128)(2,1)} async-done(((bf16[16,128,256]{2,1,0:T(8,128)(2,1)}), bf16[1,128,256]{2,1,0:T(8,128)(2,1)}) %reduce-scatter.31.cloned.1.call-update) | async-done | bytes 65552
  315.6 73.8 %reduce-scatter.33.cloned.1.call-done = bf16[1,16,2048]{2,1,0:T(8,128)(2,1)} async-done(((bf16[16,16,2048]{2,1,0:T(8,128)(2,1)}), bf16[1,16,2048]{2,1,0:T(8,128)(2,1)}) %reduce-scatter.33.cloned.1.call-update) | async-done | bytes 65552
  415.0 51.5 %reduce-scatter.35.cloned.1.call-done = bf16[1,128,352]{1,2,0:T(8,128)(2,1)} async-done(((bf16[16,128,352]{1,2,0:T(8,128)(2,1)}), bf16[1,128,352]{1,2,0:T(8,128)(2,1)}) %reduce-scatter.35.cloned.1.call-update) | async-done | bytes 90128
  467.9 75.6 %reduce-scatter.37.cloned.1.call-done = bf16[1,128,352]{1,2,0:T(8,128)(2,1)} async-done(((bf16[16,128,352]{1,2,0:T(8,128)(2,1)}), bf16[1,128,352]{1,2,0:T(8,128)(2,1)}) %reduce-scatter.37.cloned.1.call-update) | async-done | bytes 90128
  545.0 75.1 %reduce-scatter.39.cloned.1.call-done = bf16[1,22,2048]{2,1,0:T(8,128)(2,1)} async-done(((bf16[16,22,2048]{2,1,0:T(8,128)(2,1)}), bf16[1,22,2048]{2,1,0:T(8,128)(2,1)}) %reduce-scatter.39.cloned.1.call-update) | async-done | bytes 90128
  634.2 21.5 %fusion.13 = (f32[1,299056]{1,0:T(1,128)}, f32[299056]{0:T(1024)}, f32[1,299056]{1,0:T(1,128)}, f32[299056]{0:T(1024)}) fusion(f32[1,299056]{1,0:T(1,128)} %dynamic-update-slice.13, f32[1,299056]{1,0:T(1,128)} %param.27, f32[1,299056]{1,0:T(1,128)} %param.26), kind=kLoop, calls=%fused_computation.30 | loop fusion | flops 2093392 | bytes 8373568 | tf_op jit(solution)/shard_map/add | solution.py:139
  655.8 16.2 %concatenate.41 = f32[299056]{0:T(1024)} concatenate(f32[16]{0:T(128)S(1)} %bitcast.103, f32[32768]{0:T(1024)S(1)} %bitcast.93, f32[32768]{0:T(1024)S(1)} %bitcast.94, f32[32768]{0:T(1024)S(1)} %bitcast.95, f32[16]{0:T(128)S(1)} %fusion.32, f32[32768]{0:T(1024)} %bitcast.96, f32[32768]{0:T(1024)} %bitcast.97, f32[16]{0:T(128)S(1)} %bitcast.104, f32[45056]{0:T(1024)S(1)} %reshape.617, ...), dimensions={0} | concatenate | bytes 2392448 | tf_op jit(solution)/shard_map/concatenate | solution.py:137
  700.3 12.5 %fusion.16 = f32[11]{0:T(128)S(1)} fusion(f32[299056,1]{0,1:T(1,128)S(1)} %reshape.664, s32[299056]{0:T(1024)S(1)} %convert_add_fusion), kind=kOutput, calls=%fused_computation.36 | convolution fusion | flops 42765008 | bytes 2392492 | tf_op jit(solution)/shard_map/dot_general | solution.py:15
  712.7 13.0 %all-reduce.15 = (f32[11]{0:T(128)S(1)}, f32[11]{0:T(128)S(1)}) all-reduce(f32[11]{0:T(128)S(1)} %fusion.17, f32[11]{0:T(128)S(1)} %fusion.16), channel_id=1, replica_groups=mesh['dp'=16,'tensor'=8] {'tensor'}, use_global_device_ids=true, to_apply=%region_13.0 | all-reduce | flops 22 | bytes 176 | tf_op jit(solution)/shard_map/psum | solution.py:10
  725.7 38.3 %all-reduce.14 = (f32[11]{0:T(128)S(1)}, f32[11]{0:T(128)S(1)}) all-reduce(f32[11]{0:T(128)S(1)} %get-tuple-element.30, f32[11]{0:T(128)S(1)} %get-tuple-element.31), channel_id=1, replica_groups=mesh['dp'=16,'tensor'=8] {'dp'}, use_global_device_ids=true, to_apply=%region_14.0 | all-reduce | flops 22 | bytes 176 | tf_op jit(solution)/shard_map/psum | solution.py:10
  764.1 20.0 %fusion.7 = f32[299056]{0:T(1024)S(1)} fusion(s32[299056]{0:T(1024)S(1)} %convert_add_fusion, f32[11]{0:T(128)S(1)} %get-tuple-element.28, f32[11]{0:T(128)S(1)} %get-tuple-element.29), kind=kOutput, calls=%fused_computation.22 | convolution fusion | flops 42765020 | bytes 2392536 | tf_op jit(solution)/shard_map/dot_general | solution.py:145
  799.0 36.1 %all-reduce.16 = (bf16[256]{0:T(256)(128)(2,1)}, bf16[256]{0:T(256)(128)(2,1)}, bf16[256]{0:T(256)(128)(2,1)}) all-reduce(bf16[256]{0:T(256)(128)(2,1)S(1)} %dynamic-update-slice, bf16[256]{0:T(256)(128)(2,1)S(1)} %dynamic-update-slice.1, bf16[256]{0:T(256)(128)(2,1)S(1)} %dynamic-update-slice.2), channel_id=2, replica_groups=mesh['dp'=16,'tensor'=8] {'dp'}, use_global_device_ids=true, to_apply=%add | all-reduce | flops 768 | bytes 3072
  835.1 31.8 %all-gather.14.cloned.1.call-done = bf16[16,128,256]{2,1,0:T(8,128)(2,1)} async-done(((bf16[1,128,256]{2,1,0:T(8,128)(2,1)}), bf16[16,128,256]{2,1,0:T(8,128)(2,1)}) %all-gather.14.cloned.1.call-update) | async-done | bytes 1048592 | tf_op jit(solution)/shard_map/all_gather | solution.py:158
  867.0 45.1 %all-gather.16.cloned.1.call-done = bf16[16,128,256]{2,1,0:T(8,128)(2,1)} async-done(((bf16[1,128,256]{2,1,0:T(8,128)(2,1)}), bf16[16,128,256]{2,1,0:T(8,128)(2,1)}) %all-gather.16.cloned.1.call-update) | async-done | bytes 1048592 | tf_op jit(solution)/shard_map/all_gather | solution.py:159
  912.0 44.9 %all-gather.18.cloned.1.call-done = bf16[16,128,256]{2,1,0:T(8,128)(2,1)} async-done(((bf16[1,128,256]{2,1,0:T(8,128)(2,1)}), bf16[16,128,256]{2,1,0:T(8,128)(2,1)}) %all-gather.18.cloned.1.call-update) | async-done | bytes 1048592 | tf_op jit(solution)/shard_map/all_gather | solution.py:161
  957.0 45.1 %all-gather.20.cloned.1.call-done = bf16[16,16,2048]{2,1,0:T(8,128)(2,1)} async-done(((bf16[1,16,2048]{2,1,0:T(8,128)(2,1)}), bf16[16,16,2048]{2,1,0:T(8,128)(2,1)}) %all-gather.20.cloned.1.call-update) | async-done | bytes 1048592 | tf_op jit(solution)/shard_map/all_gather | solution.py:162
  1002.0 46.1 %all-gather.22.cloned.1.call-done = bf16[16,128,352]{1,2,0:T(8,128)(2,1)} async-done(((bf16[1,128,352]{1,2,0:T(8,128)(2,1)}), bf16[16,128,352]{1,2,0:T(8,128)(2,1)}) %all-gather.22.cloned.1.call-update) | async-done | bytes 1441808 | tf_op jit(solution)/shard_map/all_gather | solution.py:164
  1050.8 43.5 %all-gather.24.cloned.1.call-done = bf16[16,128,352]{1,2,0:T(8,128)(2,1)} async-done(((bf16[1,128,352]{1,2,0:T(8,128)(2,1)}), bf16[16,128,352]{1,2,0:T(8,128)(2,1)}) %all-gather.24.cloned.1.call-update) | async-done | bytes 1441808 | tf_op jit(solution)/shard_map/all_gather | solution.py:165
  1096.9 43.6 %all-gather.26.cloned.1.call-done = bf16[16,22,2048]{2,1,0:T(8,128)(2,1)} async-done(((bf16[1,22,2048]{2,1,0:T(8,128)(2,1)}), bf16[16,22,2048]{2,1,0:T(8,128)(2,1)}) %all-gather.26.cloned.1.call-update) | async-done | bytes 1441808 | tf_op jit(solution)/shard_map/all_gather | solution.py:166
  (156 shorter events, 129.3 us)
Async XLA Ops:
  7.2 133.8 %reduce-scatter.25.cloned.1.call-start = ((), (), s32[]{:S(2)}) async-start(), calls=%async_computation.16 | async-start | bytes 1114112
  7.9 154.8 %reduce-scatter.27.cloned.1.call-start = ((), (), s32[]{:S(2)}) async-start(), calls=%async_computation.17 | async-start | bytes 1114112
  8.7 229.6 %reduce-scatter.29.cloned.1.call-start = ((), (), s32[]{:S(2)}) async-start(), calls=%async_computation.18 | async-start | bytes 1114112
  9.4 304.6 %reduce-scatter.31.cloned.1.call-start = ((), (), s32[]{:S(2)}) async-start(), calls=%async_computation.19 | async-start | bytes 1114112
  10.0 379.5 %reduce-scatter.33.cloned.1.call-start = ((), (), s32[]{:S(2)}) async-start(), calls=%async_computation.20 | async-start | bytes 1114112
  10.6 455.9 %reduce-scatter.35.cloned.1.call-start = ((), (), s32[]{:S(2)}) async-start(), calls=%async_computation.21 | async-start | bytes 1531904
  12.6 530.9 %reduce-scatter.37.cloned.1.call-start = ((), (), s32[]{:S(2)}) async-start(), calls=%async_computation.22 | async-start | bytes 1531904
  15.8 604.2 %reduce-scatter.39.cloned.1.call-start = ((), (), s32[]{:S(2)}) async-start(), calls=%async_computation.23 | async-start | bytes 1671168
  18.5 816.6 %all-gather.12.cloned.1.call-start = ((), (), s32[]{:S(2)}) async-start(), calls=%async_computation.8 | async-start | bytes 1114112 | tf_op jit(solution)/shard_map/all_gather | solution.py:157
  18.7 8.7 copy-start.16
  18.7 8.8 copy-start.17
  27.7 89.5 %copy-start.14 = (u32[128]{0:T(128)S(1)}, u32[128]{0:T(128)}, u32[]{:S(2)}) copy-start(u32[128]{0:T(128)} %constant.50) | copy-start | bytes 1540
  634.2 21.5 %copy-start.13 = (bf16[1,22,2048]{2,1,0:T(8,128)(2,1)S(1)}, bf16[1,22,2048]{2,1,0:T(8,128)(2,1)}, u32[]{:S(2)}) copy-start(bf16[1,22,2048]{2,1,0:T(8,128)(2,1)} %reduce-scatter.39.cloned.1.call-done) | copy-start | bytes 270340
  634.2 21.6 %copy-start.9 = (f32[16,2,8,128]{3,1,2,0:T(2,128)S(1)}, f32[16,2,8,128]{3,1,2,0:T(2,128)}, u32[]{:S(2)}) copy-start(f32[16,2,8,128]{3,1,2,0:T(2,128)} %copy.53) | copy-start | bytes 393220
  634.2 21.6 %copy-start.10 = (f32[16,2,8,128]{3,1,2,0:T(2,128)S(1)}, f32[16,2,8,128]{3,1,2,0:T(2,128)}, u32[]{:S(2)}) copy-start(f32[16,2,8,128]{3,1,2,0:T(2,128)} %copy.54) | copy-start | bytes 393220
  764.1 20.0 %copy-start = (f32[299056]{0:T(1024)S(1)}, f32[299056]{0:T(1024)}, u32[]{:S(2)}) copy-start(f32[299056]{0:T(1024)} %get-tuple-element.41) | copy-start | bytes 3588676
  785.2 81.8 %all-gather.14.cloned.1.call-start = ((), (), s32[]{:S(2)}) async-start(), calls=%async_computation.9 | async-start | bytes 1114112 | tf_op jit(solution)/shard_map/all_gather | solution.py:158
  785.9 126.1 %all-gather.16.cloned.1.call-start = ((), (), s32[]{:S(2)}) async-start(), calls=%async_computation.10 | async-start | bytes 1114112 | tf_op jit(solution)/shard_map/all_gather | solution.py:159
  786.7 170.3 %all-gather.18.cloned.1.call-start = ((), (), s32[]{:S(2)}) async-start(), calls=%async_computation.11 | async-start | bytes 1114112 | tf_op jit(solution)/shard_map/all_gather | solution.py:161
  787.4 214.6 %all-gather.20.cloned.1.call-start = ((), (), s32[]{:S(2)}) async-start(), calls=%async_computation.12 | async-start | bytes 1114112 | tf_op jit(solution)/shard_map/all_gather | solution.py:162
  788.1 260.0 %all-gather.22.cloned.1.call-start = ((), (), s32[]{:S(2)}) async-start(), calls=%async_computation.13 | async-start | bytes 1531904 | tf_op jit(solution)/shard_map/all_gather | solution.py:164
  789.3 304.9 %all-gather.24.cloned.1.call-start = ((), (), s32[]{:S(2)}) async-start(), calls=%async_computation.14 | async-start | bytes 1531904 | tf_op jit(solution)/shard_map/all_gather | solution.py:165
  790.3 350.2 %all-gather.26.cloned.1.call-start = ((), (), s32[]{:S(2)}) async-start(), calls=%async_computation.15 | async-start | bytes 1671168 | tf_op jit(solution)/shard_map/all_gather | solution.py:166
  1096.9 46.0 %copy-start.4 = (bf16[16,128,256]{2,1,0:T(8,128)(2,1)S(1)}, bf16[16,128,256]{2,1,0:T(8,128)(2,1)}, u32[]{:S(2)}) copy-start(bf16[16,128,256]{2,1,0:T(8,128)(2,1)} %all-gather.12.cloned.1.call-done) | copy-start | bytes 3145732
  (10 other events, 23.5 us)
Sparse Core Ops, SparseCore 0:
  11.2 75.6 reduce-scatter.24
  90.4 72.2 reduce-scatter.26
  165.9 72.2 reduce-scatter.28
  241.7 72.2 reduce-scatter.30
  317.0 72.3 reduce-scatter.32
  393.4 72.9 reduce-scatter.34
  470.6 72.9 reduce-scatter.36
  547.1 72.9 reduce-scatter.38
  785.3 36.6 all-gather.11
  824.8 42.0 all-gather.13
  869.9 42.0 all-gather.15
  914.8 42.0 all-gather.17
  959.9 42.0 all-gather.19
  1004.9 43.1 all-gather.21
  1050.9 43.2 all-gather.23
  1097.1 43.3 all-gather.25
